TPU v7x, 32 devices: a whole 2x2x4 slice. The times are simulated.
32 devices in a mesh: seq: 16 (over z, y, x), head: 2 (over core).
Axes of the slice: x: 2, y: 2, z: 4, core: 2. Of those that a mesh axis runs over, the one named last changes fastest.
Arguments:
- queries: bfloat16 [1024, 1024], P('seq', 'head'), may hold values from -9 to 9
- keys: bfloat16 [2, 32768, 128], P('head', 'seq'), may hold values from -9 to 9
- values: bfloat16 [2, 32768, 128], P('head', 'seq'), may hold values from -6 to 6
- mask: int32 [8, 256], P(None, 'seq'), may hold values from 0 to 1, as said below
- out_proj: bfloat16 [1024, 4096], P('head', 'seq'), may hold values from -0.1875 to 0.1875
Outputs:
- output: bfloat16 [1024, 4096], P('seq', 'head')
Inputs may be any that keep to these rules, and one draw needn't show every extreme that they name: `mask`: each entry is 0 or 1; the share of ones differs strongly between the cached positions of different seq shards.
All inputs are finite; a program needn't handle non-finite values.
Results may differ from a plain program's by a relative error of at most 0.0057.
Values may be sent and summed in bfloat16 or wider, within the bound.
No kernel may reach another device: no remote copies, remote signals or barrier semaphores. Data moves between devices by JAX's collectives and lax.ppermute only.
A program may use at most 64 MiB of HBM per device.

v0:
```python
import jax
import jax.numpy as jnp
from jax import lax
from jax.sharding import PartitionSpec as P

BLK = 128


def on_device(queries, keys, values, mask, out_proj):
    gathered = lax.all_gather(queries, "seq", axis=0, tiled=True)
    rows = gathered.shape[0]
    head_size = keys.shape[2]
    group = gathered.shape[1] // head_size
    cached = keys.shape[1]
    query_heads = gathered.reshape(rows, group, head_size)
    key_local = keys[0]
    value_local = values[0]
    block = min(512, cached)
    count = cached // block
    mask_cols = block // BLK
    scale = 1.0 / jnp.sqrt(jnp.float32(head_size))
    offset = jnp.log(jnp.float32(cached * lax.axis_size("seq")))

    def block_sum(query_part, index, mask_part):
        start = index * block
        key_block = lax.dynamic_slice_in_dim(key_local, start, block, 0)
        value_block = lax.dynamic_slice_in_dim(value_local, start, block, 0)
        live = jnp.repeat(jnp.repeat(mask_part, BLK, axis=0), BLK, axis=1) > 0
        score = (
            jnp.einsum("qgd,kd->gqk", query_part, key_block, preferred_element_type=jnp.float32)
            * scale
            - offset
        )
        weight = jnp.where(live[None], jax.nn.sigmoid(score), 0.0).astype(jnp.bfloat16)
        return jnp.einsum("gqk,kd->qgd", weight, value_block, preferred_element_type=jnp.float32)

    def step(index, total):
        mask_part = lax.dynamic_slice_in_dim(mask, index * mask_cols, mask_cols, 1)
        return total + block_sum(query_heads, index, mask_part)

    attended = lax.fori_loop(0, count, step, jnp.zeros((rows, group, head_size), jnp.float32))
    partial_value = attended.reshape(rows, group * head_size)
    own_rows = rows // lax.axis_size("seq")
    summed = lax.psum(partial_value, "seq")
    mine = lax.dynamic_slice_in_dim(summed, lax.axis_index("seq") * own_rows, own_rows, 0)
    attended_bf = mine.astype(jnp.bfloat16)
    terms = jnp.dot(
        attended_bf,
        lax.all_gather(out_proj, "seq", axis=1, tiled=True),
        preferred_element_type=jnp.float32,
    )
    return lax.psum_scatter(terms, "head", scatter_dimension=1, tiled=True).astype(jnp.bfloat16)


def solution(mesh):
    placed = (
        P("seq", "head"),
        P("head", "seq", None),
        P("head", "seq", None),
        P(None, "seq"),
        P("head", "seq"),
    )
    return jax.shard_map(
        on_device, mesh=mesh, in_specs=placed, out_specs=P("seq", "head"), check_vma=False
    )
```

profile of v0, /device:TPU:0, one launch (start us, length us, event | category | flops | bytes accessed | tf_op | source)
XLA Modules:
  0.0 243.8 jit_solution(16637837117871356497)
XLA Ops:
  6.5 0.7 all-gather.3.cloned.1.call-update
  7.3 0.7 all-gather.5.cloned.1.call-update
  8.1 1.2 copy.6
  9.3 58.6 %all-gather.3.cloned.1.call-done = bf16[1024,512]{1,0:T(8,128)(2,1)} async-done(((bf16[64,512]{1,0:T(8,128)(2,1)}), bf16[1024,512]{1,0:T(8,128)(2,1)}) %all-gather.3.cloned.1.call-update) | async-done | bytes 1048592 | tf_op jit(solution)/shard_map/all_gather | solution.py:10
  67.9 2.1 reshape.31
  70.1 37.7 %while.16 = (s32[]{:T(128)}, f32[1024,4,128]{0,2,1:T(8,128)S(1)}, bf16[2048,128]{0,1:T(8,128)(2,1)S(1)}, s32[8,16]{1,0:T(8,128)}, bf16[2048,128]{1,0:T(8,128)(2,...) while((s32[]{:T(128)}, f32[1024,4,128]{0,2,1:T(8,128)S(1)}, ...), condition=%wide.region_1.2_spmd.clone, body=%wide.region_0.1_spmd.clone.sunk | while | flops 1089470464 | bytes 7612318 | solution.py:41
  70.1 0.8 dynamic-slice_compare_fusion.2
  70.9 3.2 %broadcast_in_dim.79 = pred[1024,4,128]{2,1,0:T(4,128)(4,1)S(1)} broadcast(pred[1024,4]{1,0:T(8,128)(4,1)S(1)} %bitcast.40), dimensions={0,1} | broadcast | bytes 528384 | tf_op jit(solution)/shard_map/while/body/eval_jaxpr/broadcast_in_dim | solution.py:28
  74.3 5.1 %bitcast_add_fusion.2 = f32[1024,4,128]{0,2,1:T(8,128)S(1)} fusion(f32[1024,4,128]{0,2,1:T(8,128)S(1)} %get-tuple-element.243, pred[1024,512]{1,0:T(8,128)(4,1)S(1)} %bitcast.41, bf16[1024,4,128]{2,1,0:T(4,128)(2,1)} %get-tuple-element.259, pred[]{:T(512)S(6)} %compare.3, bf16[2048,128]{1,0:T(8,128)(2,1)} %get-tuple-element.258, s32[]{:T(128)S(6)} %select_n.50, ...), kind=kOutput, calls=%fused_computation.4.clone.1 | convolution fusion | flops 1089470464 | bytes 6030848 | tf_op jit(solution)/shard_map/while/body/eval_jaxpr/gqk,kd->qgd/dot_general | solution.py:35
  79.5 0.8 dynamic-slice_compare_fusion.2
  80.3 3.2 %broadcast_in_dim.79 = pred[1024,4,128]{2,1,0:T(4,128)(4,1)S(1)} broadcast(pred[1024,4]{1,0:T(8,128)(4,1)S(1)} %bitcast.40), dimensions={0,1} | broadcast | bytes 528384 | tf_op jit(solution)/shard_map/while/body/eval_jaxpr/broadcast_in_dim | solution.py:28
  83.5 0.3 copy.17
  83.8 5.2 %bitcast_add_fusion.2 = f32[1024,4,128]{0,2,1:T(8,128)S(1)} fusion(f32[1024,4,128]{0,2,1:T(8,128)S(1)} %get-tuple-element.243, pred[1024,512]{1,0:T(8,128)(4,1)S(1)} %bitcast.41, bf16[1024,4,128]{2,1,0:T(4,128)(2,1)} %get-tuple-element.259, pred[]{:T(512)S(6)} %compare.3, bf16[2048,128]{1,0:T(8,128)(2,1)} %get-tuple-element.258, s32[]{:T(128)S(6)} %select_n.50, ...), kind=kOutput, calls=%fused_computation.4.clone.1 | convolution fusion | flops 1089470464 | bytes 6030848 | tf_op jit(solution)/shard_map/while/body/eval_jaxpr/gqk,kd->qgd/dot_general | solution.py:35
  89.0 0.8 dynamic-slice_compare_fusion.2
  89.8 3.2 %broadcast_in_dim.79 = pred[1024,4,128]{2,1,0:T(4,128)(4,1)S(1)} broadcast(pred[1024,4]{1,0:T(8,128)(4,1)S(1)} %bitcast.40), dimensions={0,1} | broadcast | bytes 528384 | tf_op jit(solution)/shard_map/while/body/eval_jaxpr/broadcast_in_dim | solution.py:28
  93.2 5.1 %bitcast_add_fusion.2 = f32[1024,4,128]{0,2,1:T(8,128)S(1)} fusion(f32[1024,4,128]{0,2,1:T(8,128)S(1)} %get-tuple-element.243, pred[1024,512]{1,0:T(8,128)(4,1)S(1)} %bitcast.41, bf16[1024,4,128]{2,1,0:T(4,128)(2,1)} %get-tuple-element.259, pred[]{:T(512)S(6)} %compare.3, bf16[2048,128]{1,0:T(8,128)(2,1)} %get-tuple-element.258, s32[]{:T(128)S(6)} %select_n.50, ...), kind=kOutput, calls=%fused_computation.4.clone.1 | convolution fusion | flops 1089470464 | bytes 6030848 | tf_op jit(solution)/shard_map/while/body/eval_jaxpr/gqk,kd->qgd/dot_general | solution.py:35
  98.4 0.8 dynamic-slice_compare_fusion.2
  99.2 3.2 %broadcast_in_dim.79 = pred[1024,4,128]{2,1,0:T(4,128)(4,1)S(1)} broadcast(pred[1024,4]{1,0:T(8,128)(4,1)S(1)} %bitcast.40), dimensions={0,1} | broadcast | bytes 528384 | tf_op jit(solution)/shard_map/while/body/eval_jaxpr/broadcast_in_dim | solution.py:28
  102.4 0.3 copy.17
  102.6 5.1 %bitcast_add_fusion.2 = f32[1024,4,128]{0,2,1:T(8,128)S(1)} fusion(f32[1024,4,128]{0,2,1:T(8,128)S(1)} %get-tuple-element.243, pred[1024,512]{1,0:T(8,128)(4,1)S(1)} %bitcast.41, bf16[1024,4,128]{2,1,0:T(4,128)(2,1)} %get-tuple-element.259, pred[]{:T(512)S(6)} %compare.3, bf16[2048,128]{1,0:T(8,128)(2,1)} %get-tuple-element.258, s32[]{:T(128)S(6)} %select_n.50, ...), kind=kOutput, calls=%fused_computation.4.clone.1 | convolution fusion | flops 1089470464 | bytes 6030848 | tf_op jit(solution)/shard_map/while/body/eval_jaxpr/gqk,kd->qgd/dot_general | solution.py:35
  107.8 116.3 %all-reduce.1 = bf16[1024,512]{0,1:T(8,128)(2,1)S(1)} all-reduce(f32[1024,512]{0,1:T(8,128)S(1)} %bitcast.42), channel_id=1, replica_groups=mesh['seq'=16,'head'=2] {'seq'}, use_global_device_ids=true, to_apply=%region_2.3 | all-reduce | flops 524288 | bytes 3145728 | tf_op jit(solution)/shard_map/psum | solution.py:44
  224.1 4.1 %fusion.21 = f32[64,4096]{1,0:T(8,128)} fusion(bf16[512,4096]{1,0:T(8,128)(2,1)} %all-gather.5.cloned.1.call-done, bf16[1024,512]{0,1:T(8,128)(2,1)S(1)} %all-reduce.1, s32[]{:T(128)S(6)} %select_n.35), kind=kOutput, calls=%fused_computation.18 | convolution fusion | flops 268435456 | bytes 5373956 | tf_op jit(solution)/shard_map/dot_general | solution.py:47
  228.3 7.3 %reduce-scatter.2.cloned.1.call-done = f32[64,2048]{1,0:T(8,128)} async-done(((f32[64,4096]{1,0:T(8,128)}), f32[64,2048]{1,0:T(8,128)}) %reduce-scatter.2.cloned.1.call-update) | async-done | bytes 524304 | tf_op jit(solution)/shard_map/reduce_scatter | solution.py:52
  235.5 1.8 convert_element_type.17
  (12 shorter events, 0.8 us)
Async XLA Ops:
  6.5 61.4 %all-gather.3.cloned.1.call-start = ((), (), s32[]{:S(2)}) async-start(), calls=%async_computation.1 | async-start | bytes 1114112 | tf_op jit(solution)/shard_map/all_gather | solution.py:10
  7.3 216.9 %all-gather.5.cloned.1.call-start = ((), (), s32[]{:S(2)}) async-start(), calls=%async_computation.2 | async-start | bytes 4456448 | tf_op jit(solution)/shard_map/all_gather | solution.py:49
  8.0 227.5 %reduce-scatter.2.cloned.1.call-start = ((), (), s32[]{:S(2)}) async-start(), calls=%async_computation.3 | async-start | bytes 1572864 | tf_op jit(solution)/shard_map/reduce_scatter | solution.py:52
Sparse Core Ops, SparseCore 0:
  10.1 57.7 all-gather.2
  70.7 100.2 all-gather.4
  228.4 7.0 reduce-scatter.1
where the time goes:
time: 244 us
  blocking collectives  116 us (48%)
  waiting for transfers between devices  67.3 us (28%)
  matrix products  24.7 us (10%)
  local copies, waits for them, and re-layouts  17.3 us (7%)
  between operations  13.2 us (5%)
  other arithmetic  4.83 us (2%)
    psum x1, blocking collectives, on_device(): summed = lax.psum(partial_value, 'seq')  116 us
    all_gather x1, waiting for transfers between devices, on_device(): gathered = lax.all_gather(queries, 'seq', axis=0, tiled=True)  58.6 us
    dot_general x4, matrix products, block_sum(): jnp.einsum('gqk,kd->qgd', weight, value_block, preferred_element_type=jnp...  20.6 us
    broadcast_in_dim x8, local copies, waits for them, and re-layouts, block_sum(): live = jnp.repeat(jnp.repeat(mask_part, BLK, axis=0), BLK, axis=1) > 0  12.9 us
    reduce_scatter x1, waiting for transfers between devices, on_device(): lax.psum_scatter(terms, 'head', scatter_dimension=1, tiled=True)  7.26 us
  transfers between devices with their start and end apart: 3, of which 2 were waited for; matrix products, arithmetic and copies ran while one was open for 17% of the time, Pallas kernels for 0%

commit v1 on v0

--- a/solution.py
+++ b/solution.py
@@ -6,8 +6,31 @@
 BLK = 128
 
 
+def plate_launch(buf, dim_i):
+    formed = list(buf.shape[1:])
+    formed[dim_i] *= buf.shape[0]
+    now = jnp.moveaxis(buf, 0, dim_i).reshape(formed)
+    return now
+
+
+def quotas_reach(original, peer_axis):
+    val2, taken_in = (jax.lax.psum(1, peer_axis), jax.lax.axis_index(peer_axis))
+    res, x_now = (original[None], 1)
+    while x_now < val2:
+        near = jax.lax.ppermute(res, peer_axis, [(i, i ^ x_now) for i in range(val2)])
+        side_arr = taken_in & x_now == 0
+        res = jnp.concatenate([jnp.where(side_arr, res, near), jnp.where(side_arr, near, res)])
+        x_now *= 2
+    return res
+
+
 def on_device(queries, keys, values, mask, out_proj):
-    gathered = lax.all_gather(queries, "seq", axis=0, tiled=True)
+
+    def _scan_windows(axis_k, x_local, my_data):
+        r_now = plate_launch(quotas_reach(my_data, x_local), axis_k)
+        return r_now
+
+    gathered = _scan_windows(0, "seq", queries)
     rows = gathered.shape[0]
     head_size = keys.shape[2]
     group = gathered.shape[1] // head_size

time: 244 us -> 218 us (0.89)
  waiting for transfers between devices: 67.3 us -> 38.2 us
  starting transfers between devices: 0.08 us -> 10.3 us
  blocking collectives: 116 us -> 109 us
    all_gather x1 -> x0, waiting for transfers between devices: 58.6 us -> none  [on_device(): gathered = lax.all_gather(queries, 'seq', axis=0, tiled=True)]
    ppermute x0 -> x4, waiting for transfers between devices: none -> 30.7 us  [quotas_reach(): jax.lax.ppermute(res, peer_axis, [(i, i ^ x_now) for i in range(val2)])]
    ppermute x0 -> x4, starting transfers between devices: none -> 10.3 us  [quotas_reach(): jax.lax.ppermute(res, peer_axis, [(i, i ^ x_now) for i in range(val2)])]
    psum x1, blocking collectives: 116 us -> 109 us  [on_device(): summed = lax.psum(partial_value, 'seq')]
    gt x4, other arithmetic: 3.06 us -> 0.31 us  [block_sum(): live = jnp.repeat(jnp.repeat(mask_part, BLK, axis=0), BLK, axis=1) > 0]
  transfers between devices with their start and end apart: 3 -> 6, of which waited for: 2 -> 5; matrix products, arithmetic and copies ran while one was open for 17% -> 18% of each run, Pallas kernels for 0% -> 0%
where the time goes in v1:
time: 218 us; the launch traced here: 217 us
  blocking collectives  109 us (50%)
  waiting for transfers between devices  38.2 us (18%)
  matrix products  25 us (11%)
  local copies, waits for them, and re-layouts  17.1 us (8%)
  between operations  13.5 us (6%)
  starting transfers between devices  10.3 us (5%)
  other arithmetic  4.05 us (2%)
    psum x1, blocking collectives, on_device(): summed = lax.psum(partial_value, 'seq')  109 us
    ppermute x4, waiting for transfers between devices, quotas_reach(): jax.lax.ppermute(res, peer_axis, [(i, i ^ x_now) for i in range(val2)])  30.7 us
    dot_general x4, matrix products, block_sum(): jnp.einsum('gqk,kd->qgd', weight, value_block, preferred_element_type=jnp...  20.9 us
    broadcast_in_dim x8, local copies, waits for them, and re-layouts, block_sum(): live = jnp.repeat(jnp.repeat(mask_part, BLK, axis=0), BLK, axis=1) > 0  12.9 us
    ppermute x4, starting transfers between devices, quotas_reach(): jax.lax.ppermute(res, peer_axis, [(i, i ^ x_now) for i in range(val2)])  10.3 us
    reduce_scatter x1, waiting for transfers between devices, on_device(): lax.psum_scatter(terms, 'head', scatter_dimension=1, tiled=True)  7.43 us
  transfers between devices with their start and end apart: 6, of which 5 were waited for; matrix products, arithmetic and copies ran while one was open for 18% of the time, Pallas kernels for 0%

profile of v1, /device:TPU:0, one launch (start us, length us, event | category | flops | bytes accessed | tf_op | source)
XLA Modules:
  0.0 217.5 jit_solution(5366662287644767438)
XLA Ops:
  6.5 3.0 %collective-permute-start = (bf16[1,64,512]{2,1,0:T(8,128)(2,1)}, bf16[1,64,512]{2,1,0:T(8,128)(2,1)S(1)}, u32[]{:S(2)}, u32[]{:S(2)}) collective-permute-start(bf16[1,64,512]{2,1,0:T(8,128)(2,1)} %bitcast.47), channel_id=1, source_target_pairs={{0,2},{2,0},{4,6},{6,4},{8,10},{10,8},{12,14},{14,12},{16,18},{18,... | collective-permute-start | bytes 196616 | tf_op jit(solution)/shard_map/ppermute | solution.py:20
  9.5 2.5 %collective-permute-done = bf16[1,64,512]{2,1,0:T(8,128)(2,1)S(1)} collective-permute-done((bf16[1,64,512]{2,1,0:T(8,128)(2,1)}, bf16[1,64,512]{2,1,0:T(8,128)(2,1)S(1)}, u32[]{:S(2)}, u32[]{:S(2)}) %collective-permute-start) | collective-permute-done | bytes 65568 | tf_op jit(solution)/shard_map/ppermute | solution.py:20
  12.0 0.9 broadcast_select_fusion.7
  12.8 2.1 collective-permute-start.1
  15.0 2.9 %collective-permute-done.1 = bf16[2,64,512]{2,1,0:T(8,128)(2,1)S(1)} collective-permute-done((bf16[2,64,512]{2,1,0:T(8,128)(2,1)S(1)}, bf16[2,64,512]{2,1,0:T(8,128)(2,1)S(1)}, u32[]{:S(2)}, u32[]{:S(2)}) %collective-permute-start.1) | collective-permute-done | bytes 131104 | tf_op jit(solution)/shard_map/ppermute | solution.py:20
  18.0 2.1 collective-permute-start.2
  20.1 4.4 %collective-permute-done.2 = bf16[4,64,512]{2,1,0:T(8,128)(2,1)S(1)} collective-permute-done((bf16[4,64,512]{2,1,0:T(8,128)(2,1)S(1)}, bf16[4,64,512]{2,1,0:T(8,128)(2,1)S(1)}, u32[]{:S(2)}, u32[]{:S(2)}) %collective-permute-start.2) | collective-permute-done | bytes 262176 | tf_op jit(solution)/shard_map/ppermute | solution.py:20
  25.4 3.0 %collective-permute-start.3 = (bf16[8,64,512]{2,1,0:T(8,128)(2,1)}, bf16[8,64,512]{2,1,0:T(8,128)(2,1)S(1)}, u32[]{:S(2)}, u32[]{:S(2)}) collective-permute-start(bf16[8,64,512]{2,1,0:T(8,128)(2,1)} %pad_maximum_fusion.1), channel_id=1, source_target_pairs={{0,16},{2,18},{4,20},{6,22},{8,24},{10,26},{12,28},{14,30},{16,0},... | collective-permute-start | bytes 1572872 | tf_op jit(solution)/shard_map/ppermute | solution.py:20
  28.5 2.1 copy.6
  30.6 20.9 %collective-permute-done.3 = bf16[8,64,512]{2,1,0:T(8,128)(2,1)S(1)} collective-permute-done((bf16[8,64,512]{2,1,0:T(8,128)(2,1)}, bf16[8,64,512]{2,1,0:T(8,128)(2,1)S(1)}, u32[]{:S(2)}, u32[]{:S(2)}) %collective-permute-start.3) | collective-permute-done | bytes 524320 | tf_op jit(solution)/shard_map/ppermute | solution.py:20
  51.7 1.1 reshape_reshape.3
  52.8 35.3 %while.16 = (s32[]{:T(128)}, f32[1024,4,128]{0,2,1:T(8,128)S(1)}, bf16[2048,128]{0,1:T(8,128)(2,1)}, s32[8,16]{1,0:T(8,128)S(1)}, bf16[2048,128]{1,0:T(8,128)(2,...) while((s32[]{:T(128)}, f32[1024,4,128]{0,2,1:T(8,128)S(1)}, ...), condition=%wide.region_1.2_spmd.clone, body=%wide.region_0.1_spmd.clone.sunk | while | flops 1089470464 | bytes 7612318 | solution.py:64
  52.9 3.2 %broadcast_in_dim.83 = pred[1024,4,128]{2,1,0:T(4,128)(4,1)S(1)} broadcast(pred[1024,4]{1,0:T(8,128)(4,1)S(1)} %bitcast.43), dimensions={0,1} | broadcast | bytes 528384 | tf_op jit(solution)/shard_map/while/body/eval_jaxpr/broadcast_in_dim | solution.py:51
  56.4 5.2 %bitcast_add_fusion.2 = f32[1024,4,128]{0,2,1:T(8,128)S(1)} fusion(f32[1024,4,128]{0,2,1:T(8,128)S(1)} %get-tuple-element.251, pred[1024,512]{1,0:T(8,128)(4,1)S(1)} %bitcast.44, bf16[1024,4,128]{2,1,0:T(4,128)(2,1)} %get-tuple-element.267, pred[]{:T(512)S(6)} %compare.3, bf16[2048,128]{1,0:T(8,128)(2,1)} %get-tuple-element.266, s32[]{:T(128)S(6)} %select_n.126, ...), kind=kOutput, calls=%fused_computation.4.clone.1 | convolution fusion | flops 1089470464 | bytes 6030848 | tf_op jit(solution)/shard_map/while/body/eval_jaxpr/gqk,kd->qgd/dot_general | solution.py:58
  61.7 3.2 %broadcast_in_dim.83 = pred[1024,4,128]{2,1,0:T(4,128)(4,1)S(1)} broadcast(pred[1024,4]{1,0:T(8,128)(4,1)S(1)} %bitcast.43), dimensions={0,1} | broadcast | bytes 528384 | tf_op jit(solution)/shard_map/while/body/eval_jaxpr/broadcast_in_dim | solution.py:51
  65.2 5.2 %bitcast_add_fusion.2 = f32[1024,4,128]{0,2,1:T(8,128)S(1)} fusion(f32[1024,4,128]{0,2,1:T(8,128)S(1)} %get-tuple-element.251, pred[1024,512]{1,0:T(8,128)(4,1)S(1)} %bitcast.44, bf16[1024,4,128]{2,1,0:T(4,128)(2,1)} %get-tuple-element.267, pred[]{:T(512)S(6)} %compare.3, bf16[2048,128]{1,0:T(8,128)(2,1)} %get-tuple-element.266, s32[]{:T(128)S(6)} %select_n.126, ...), kind=kOutput, calls=%fused_computation.4.clone.1 | convolution fusion | flops 1089470464 | bytes 6030848 | tf_op jit(solution)/shard_map/while/body/eval_jaxpr/gqk,kd->qgd/dot_general | solution.py:58
  70.5 3.2 %broadcast_in_dim.83 = pred[1024,4,128]{2,1,0:T(4,128)(4,1)S(1)} broadcast(pred[1024,4]{1,0:T(8,128)(4,1)S(1)} %bitcast.43), dimensions={0,1} | broadcast | bytes 528384 | tf_op jit(solution)/shard_map/while/body/eval_jaxpr/broadcast_in_dim | solution.py:51
  74.0 5.2 %bitcast_add_fusion.2 = f32[1024,4,128]{0,2,1:T(8,128)S(1)} fusion(f32[1024,4,128]{0,2,1:T(8,128)S(1)} %get-tuple-element.251, pred[1024,512]{1,0:T(8,128)(4,1)S(1)} %bitcast.44, bf16[1024,4,128]{2,1,0:T(4,128)(2,1)} %get-tuple-element.267, pred[]{:T(512)S(6)} %compare.3, bf16[2048,128]{1,0:T(8,128)(2,1)} %get-tuple-element.266, s32[]{:T(128)S(6)} %select_n.126, ...), kind=kOutput, calls=%fused_computation.4.clone.1 | convolution fusion | flops 1089470464 | bytes 6030848 | tf_op jit(solution)/shard_map/while/body/eval_jaxpr/gqk,kd->qgd/dot_general | solution.py:58
  79.3 3.2 %broadcast_in_dim.83 = pred[1024,4,128]{2,1,0:T(4,128)(4,1)S(1)} broadcast(pred[1024,4]{1,0:T(8,128)(4,1)S(1)} %bitcast.43), dimensions={0,1} | broadcast | bytes 528384 | tf_op jit(solution)/shard_map/while/body/eval_jaxpr/broadcast_in_dim | solution.py:51
  82.8 5.3 %bitcast_add_fusion.2 = f32[1024,4,128]{0,2,1:T(8,128)S(1)} fusion(f32[1024,4,128]{0,2,1:T(8,128)S(1)} %get-tuple-element.251, pred[1024,512]{1,0:T(8,128)(4,1)S(1)} %bitcast.44, bf16[1024,4,128]{2,1,0:T(4,128)(2,1)} %get-tuple-element.267, pred[]{:T(512)S(6)} %compare.3, bf16[2048,128]{1,0:T(8,128)(2,1)} %get-tuple-element.266, s32[]{:T(128)S(6)} %select_n.126, ...), kind=kOutput, calls=%fused_computation.4.clone.1 | convolution fusion | flops 1089470464 | bytes 6030848 | tf_op jit(solution)/shard_map/while/body/eval_jaxpr/gqk,kd->qgd/dot_general | solution.py:58
  88.1 109.2 %all-reduce.1 = bf16[1024,512]{0,1:T(8,128)(2,1)S(1)} all-reduce(f32[1024,512]{0,1:T(8,128)S(1)} %bitcast.45), channel_id=1, replica_groups=mesh['seq'=16,'head'=2] {'seq'}, use_global_device_ids=true, to_apply=%region_2.3 | all-reduce | flops 524288 | bytes 3145728 | tf_op jit(solution)/shard_map/psum | solution.py:67
  197.3 4.1 %fusion.21 = f32[64,4096]{1,0:T(8,128)} fusion(bf16[512,4096]{1,0:T(8,128)(2,1)} %all-gather.2.cloned.1.call-done, bf16[1024,512]{0,1:T(8,128)(2,1)S(1)} %all-reduce.1, s32[]{:T(128)S(6)} %select_n.95), kind=kOutput, calls=%fused_computation.25 | convolution fusion | flops 268435456 | bytes 5373956 | tf_op jit(solution)/shard_map/dot_general | solution.py:70
  201.4 7.4 %reduce-scatter.2.cloned.1.call-done = f32[64,2048]{1,0:T(8,128)} async-done(((f32[64,4096]{1,0:T(8,128)}), f32[64,2048]{1,0:T(8,128)}) %reduce-scatter.2.cloned.1.call-update) | async-done | bytes 524304 | tf_op jit(solution)/shard_map/reduce_scatter | solution.py:75
  208.9 1.8 convert_element_type.17
  (27 shorter events, 2.7 us)
Async XLA Ops:
  6.5 190.8 %all-gather.2.cloned.1.call-start = ((), (), s32[]{:S(2)}) async-start(), calls=%async_computation.1 | async-start | bytes 4456448 | tf_op jit(solution)/shard_map/all_gather | solution.py:72
  6.5 5.4 %collective-permute-start = (bf16[1,64,512]{2,1,0:T(8,128)(2,1)}, bf16[1,64,512]{2,1,0:T(8,128)(2,1)S(1)}, u32[]{:S(2)}, u32[]{:S(2)}) collective-permute-start(bf16[1,64,512]{2,1,0:T(8,128)(2,1)} %bitcast.47), channel_id=1, source_target_pairs={{0,2},{2,0},{4,6},{6,4},{8,10},{10,8},{12,14},{14,12},{16,18},{18,... | collective-permute-start | bytes 196616 | tf_op jit(solution)/shard_map/ppermute | solution.py:20
  12.8 5.1 %collective-permute-start.1 = (bf16[2,64,512]{2,1,0:T(8,128)(2,1)S(1)}, bf16[2,64,512]{2,1,0:T(8,128)(2,1)S(1)}, u32[]{:S(2)}, u32[]{:S(2)}) collective-permute-start(bf16[2,64,512]{2,1,0:T(8,128)(2,1)S(1)} %pad_maximum_fusion.3), channel_id=1, source_target_pairs={{0,4},{2,6},{4,0},{6,2},{8,12},{10,14},{12,8},{14,10},{16,20},{18,... | collective-permute-start | bytes 393224 | tf_op jit(solution)/shard_map/ppermute | solution.py:20
  18.0 6.5 %collective-permute-start.2 = (bf16[4,64,512]{2,1,0:T(8,128)(2,1)S(1)}, bf16[4,64,512]{2,1,0:T(8,128)(2,1)S(1)}, u32[]{:S(2)}, u32[]{:S(2)}) collective-permute-start(bf16[4,64,512]{2,1,0:T(8,128)(2,1)S(1)} %pad_maximum_fusion.2), channel_id=1, source_target_pairs={{0,8},{2,10},{4,12},{6,14},{8,0},{10,2},{12,4},{14,6},{16,24},{18,... | collective-permute-start | bytes 786440 | tf_op jit(solution)/shard_map/ppermute | solution.py:20
  24.5 28.3 %copy-start = (s32[8,16]{1,0:T(8,128)S(1)}, s32[8,16]{1,0:T(8,128)}, u32[]{:S(2)}) copy-start(s32[8,16]{1,0:T(8,128)} %param.10) | copy-start | bytes 1540
  25.4 26.1 %collective-permute-start.3 = (bf16[8,64,512]{2,1,0:T(8,128)(2,1)}, bf16[8,64,512]{2,1,0:T(8,128)(2,1)S(1)}, u32[]{:S(2)}, u32[]{:S(2)}) collective-permute-start(bf16[8,64,512]{2,1,0:T(8,128)(2,1)} %pad_maximum_fusion.1), channel_id=1, source_target_pairs={{0,16},{2,18},{4,20},{6,22},{8,24},{10,26},{12,28},{14,30},{16,0},... | collective-permute-start | bytes 1572872 | tf_op jit(solution)/shard_map/ppermute | solution.py:20
  28.4 180.4 %reduce-scatter.2.cloned.1.call-start = ((), (), s32[]{:S(2)}) async-start(), calls=%async_computation.2 | async-start | bytes 1572864 | tf_op jit(solution)/shard_map/reduce_scatter | solution.py:75
Sparse Core Ops, SparseCore 0:
  28.6 103.7 all-gather.1
  201.6 7.2 reduce-scatter.1
